TPU v7x, 256 devices: a whole 4x4x8 slice. The times are simulated.
256 devices in a mesh: dp: 16 (over x, y_lo, core), fsdp: 16 (over z, y_hi).
Axes of the slice: x: 4, y: 4 (y_hi: 2, y_lo: 2; y = y_hi * 2 + y_lo), z: 8, core: 2. Of those that a mesh axis runs over, the one named last changes fastest.
Arguments:
- fields: bfloat16 [16, 6, 48, 48, 48, 128], P('dp', None, 'fsdp'), may hold values from -6 to 6
- targets: bfloat16 [16, 6, 48, 2304], P('dp', None, 'fsdp'), may hold values from -6 to 6
- lists: int32 [16, 6], P('dp'), may hold values from 0 to 5, each once within a row
- counts: int32 [16], replicated, may hold values from 1 to 6, as said below
- spectral_w: bfloat16 [32, 2, 128, 128], P('fsdp'), may hold values from -0.375 to 0.375
- local_w: bfloat16 [128, 128], replicated, may hold values from -0.5 to 0.5
- proj: float32 [128], replicated, may hold values from -0.5 to 0.5
Outputs:
- grad_spectral: float32 [32, 2, 128, 128], P('fsdp')
- grad_local: float32 [128, 128], replicated
Inputs may be any that keep to these rules, and one draw needn't show every extreme that they name: Each row of lists names every slot of its lane once; the first counts[l] entries of row l are lane l's live grids. `counts`: exactly one lane has 6 live grids; every other lane has 1 or 2.
All inputs are finite; a program needn't handle non-finite values.
Results may differ from a plain program's by a relative error of at most 0.0036.
The roundings to bfloat16 on the way count: a program that leaves them out, or rounds other values in their place, can miss the bound.
Values may be sent and summed in bfloat16 or wider, within the bound.
A program may use at most 64 MiB of HBM per device.

v0:
```python
import math
import jax
import jax.numpy as jnp
from jax import lax
from jax.sharding import PartitionSpec as P

MX = 4
MY = 4
MZ = 2
highest = lax.Precision.HIGHEST
root_half = 0.7071067811865476
inv_root_two_pi = 0.3989422804014327


def phase_table(mode_ids, cell_ids, length, direction):
    product = mode_ids[:, None] * cell_ids[None, :] % length
    angle = product.astype(jnp.float32) * (2.0 * math.pi / length)
    return (jnp.cos(angle), direction * jnp.sin(angle))


def mode_lists():
    kx_ids = jnp.arange(MX, dtype=jnp.int32) - MX // 2
    ky_ids = jnp.arange(MY, dtype=jnp.int32) - MY // 2
    kz_ids = jnp.arange(MZ, dtype=jnp.int32)
    return (kx_ids, ky_ids, kz_ids)


def complex_contract(real_part, imag_part, cos_t, sin_t, form):

    def product(left, right):
        return jnp.einsum(form, left, right, precision=highest)

    return (
        product(real_part, cos_t) - product(imag_part, sin_t),
        product(real_part, sin_t) + product(imag_part, cos_t),
    )


def forward_modes(grid_field, x_cells, scale):
    grid_len = grid_field.shape[1]
    kx_ids, ky_ids, kz_ids = mode_lists()
    cells = jnp.arange(grid_len, dtype=jnp.int32)
    cos_z, sin_z = phase_table(kz_ids, cells, grid_len, -1.0)
    part_re = jnp.einsum(
        "abzc,kz->abkc", grid_field, cos_z.astype(jnp.bfloat16), preferred_element_type=jnp.float32
    )
    part_im = jnp.einsum(
        "abzc,kz->abkc", grid_field, sin_z.astype(jnp.bfloat16), preferred_element_type=jnp.float32
    )
    cos_y, sin_y = phase_table(ky_ids, cells, grid_len, -1.0)
    next_re, next_im = complex_contract(part_re, part_im, cos_y, sin_y, "abkc,jb->ajkc")
    cos_x, sin_x = phase_table(kx_ids, x_cells, grid_len, -1.0)
    last_re, last_im = complex_contract(next_re, next_im, cos_x, sin_x, "ajkc,ia->ijkc")
    stacked = jnp.stack([last_re, last_im], axis=3) * scale
    return stacked.reshape(MX * MY * MZ, 2, stacked.shape[-1])


def inverse_modes(spectrum, x_cells, grid_len):
    kx_ids, ky_ids, kz_ids = mode_lists()
    cells = jnp.arange(grid_len, dtype=jnp.int32)
    values = spectrum.astype(jnp.float32).reshape(MX, MY, MZ, 2, spectrum.shape[-1])
    cos_x, sin_x = phase_table(kx_ids, x_cells, grid_len, 1.0)
    first_re, first_im = complex_contract(
        values[:, :, :, 0], values[:, :, :, 1], cos_x, sin_x, "ijkc,ia->ajkc"
    )
    cos_y, sin_y = phase_table(ky_ids, cells, grid_len, 1.0)
    second_re, second_im = complex_contract(first_re, first_im, cos_y, sin_y, "ajkc,jb->abkc")
    cos_z, sin_z = phase_table(kz_ids, cells, grid_len, 1.0)
    real_out = jnp.einsum("abkc,kz->abzc", second_re, cos_z, precision=highest)
    real_out = real_out - jnp.einsum("abkc,kz->abzc", second_im, sin_z, precision=highest)
    return real_out * float(MX * MY * MZ) ** (-0.5)


def mix_modes(coeff_b, weights):
    signs = jnp.array([1.0, -1.0], jnp.bfloat16).reshape(1, 2, 1, 1)
    spec_re = jnp.einsum(
        "gmri,mrio->gmo", coeff_b, weights * signs, preferred_element_type=jnp.float32
    )
    spec_im = jnp.einsum(
        "gmri,mrio->gmo", coeff_b[:, :, ::-1], weights, preferred_element_type=jnp.float32
    )
    return jnp.stack([spec_re, spec_im], axis=2)


def weight_grad(coeff_b, back_stack):
    coeff_f = coeff_b.astype(jnp.float32)
    rotated = jnp.stack([-coeff_f[:, :, 1], coeff_f[:, :, 0]], axis=2)
    grad_re = jnp.einsum("gmri,gmro->mio", coeff_f, back_stack, precision=highest)
    grad_im = jnp.einsum("gmri,gmro->mio", rotated, back_stack, precision=highest)
    return jnp.stack([grad_re, grad_im], axis=1)


def point_part(grid_field, branch, local_w, proj, grid_target, scale):
    width = grid_field.shape[-1]
    flat_field = grid_field.reshape(-1, width)
    pre = branch.reshape(-1, width) + jnp.dot(
        flat_field, local_w, preferred_element_type=jnp.float32
    )
    erf_part = lax.erf(pre * root_half)
    active = 0.5 * pre * (1.0 + erf_part)
    pred = jnp.dot(active, proj, precision=highest)
    resid = (pred - grid_target.reshape(-1).astype(jnp.float32)) * scale
    slope = 0.5 * (1.0 + erf_part) + pre * jnp.exp(-0.5 * pre * pre) * inv_root_two_pi
    d_pre = (resid[:, None] * proj[None, :] * slope).astype(jnp.bfloat16)
    local_grad = lax.dot_general(
        flat_field, d_pre, (((0,), (0,)), ((), ())), preferred_element_type=jnp.float32
    )
    return (d_pre.reshape(grid_field.shape), local_grad)


def body(fields, targets, lists, counts, spectral_w, local_w, proj):
    grid_store = fields[0]
    target_store = targets[0]
    slot_order = lists[0]
    slot_count = grid_store.shape[0]
    plane_count = grid_store.shape[1]
    grid_len = grid_store.shape[2]
    width = grid_store.shape[-1]
    lane_index = lax.axis_index("dp")
    x_cells = lax.axis_index("fsdp") * plane_count + jnp.arange(plane_count, dtype=jnp.int32)
    scale = 1.0 / jnp.sum(counts).astype(jnp.float32)
    mode_scale = float(MX * MY * MZ) ** (-0.5)
    full_weights = lax.all_gather(spectral_w, "fsdp", axis=0, tiled=True)
    live_count = counts[lane_index]
    coeff_init = jnp.zeros((slot_count, MX * MY * MZ, 2, width), jnp.float32)

    def forward_pass(position, coeff_stack):
        slot_index = slot_order[position]
        grid_field = lax.dynamic_index_in_dim(grid_store, slot_index, 0, keepdims=False)
        grid_coeff = forward_modes(grid_field, x_cells, float(grid_len) ** (-1.5))
        return lax.dynamic_update_index_in_dim(coeff_stack, grid_coeff, position, 0)

    coeff_stack = lax.fori_loop(0, live_count, forward_pass, coeff_init)
    full_coeff = lax.psum(coeff_stack, "fsdp")
    coeff_b = full_coeff.astype(jnp.bfloat16)
    spectrum = mix_modes(coeff_b, full_weights).astype(jnp.bfloat16)

    def backward_pass(position, carry):
        back_stack, local_total = carry
        slot_index = slot_order[position]
        grid_field = lax.dynamic_index_in_dim(grid_store, slot_index, 0, keepdims=False)
        grid_target = lax.dynamic_index_in_dim(target_store, slot_index, 0, keepdims=False)
        grid_spectrum = lax.dynamic_index_in_dim(spectrum, position, 0, keepdims=False)
        branch = inverse_modes(grid_spectrum, x_cells, grid_len)
        d_pre, local_grad = point_part(grid_field, branch, local_w, proj, grid_target, scale)
        grid_back = forward_modes(d_pre, x_cells, mode_scale)
        return (
            lax.dynamic_update_index_in_dim(back_stack, grid_back, position, 0),
            local_total + local_grad,
        )

    back_init = (jnp.zeros_like(coeff_init), jnp.zeros((width, width), jnp.float32))
    back_stack, local_total = lax.fori_loop(0, live_count, backward_pass, back_init)
    grad_part = lax.psum_scatter(
        weight_grad(coeff_b, back_stack), "fsdp", scatter_dimension=0, tiled=True
    )
    grad_spectral = lax.psum(grad_part, "dp")
    grad_local = lax.psum(local_total, ("dp", "fsdp"))
    return (grad_spectral, grad_local)


def solution(mesh):
    return jax.shard_map(
        body,
        mesh=mesh,
        in_specs=(
            P("dp", None, "fsdp", None, None, None),
            P("dp", None, "fsdp", None),
            P("dp", None),
            P(),
            P("fsdp", None, None, None),
            P(),
            P(),
        ),
        out_specs=(P("fsdp", None, None, None), P()),
        check_vma=False,
    )
```

profile of v0, /device:TPU:1, one launch (start us, length us, event | category | flops | bytes accessed | tf_op | source)
XLA Modules:
  0.0 955.1 jit_solution(6195922219674476142)
XLA Ops:
  7.9 1.2 dynamic_slice.42
  9.2 11.0 %while.28 = (s32[]{:T(128)}, f32[6,32,2,128]{3,0,2,1:T(8,128)S(1)}, s32[]{:T(128)}, s32[6]{0:T(128)}, bf16[6,3,48,48,128]{4,3,2,1,0:T(8,128)(2,1)}, /*index=5*/s32[]{:T(128)}, s32[]{:T(128)}, s32[]{:T(128)}, s32[]{:T(128)}) while((s32[]{:T(128)}, f32[6,32,2,128]{3,0,2,1:T(8,128)S(1)}, s32[]{:T(128)}, s32[6]{0:T(128)}, ...), condition=%wide.region_1.2_spmd.clone, body=%wide.region_0.0_spmd.clone.sunk | while | flops 14786103 | bytes 4907401 | solution.py:133
  9.9 1.3 dynamic_slice.73
  13.2 1.9 fusion.419
  15.4 1.9 fusion.421
  21.0 70.4 %all-reduce.11 = bf16[6,32,2,128]{3,0,2,1:T(8,128)(2,1)S(1)} all-reduce(f32[6,32,2,128]{3,0,2,1:T(8,128)S(1)} %get-tuple-element.239), channel_id=1, replica_groups=mesh['dp'=16,'fsdp'=16] {'fsdp'}, use_global_device_ids=true, to_apply=%region_2.3 | all-reduce | flops 49152 | bytes 294912 | tf_op jit(solution)/shard_map/psum | solution.py:134
  92.3 5.5 all-gather.2.cloned.1.call-done
  97.7 2.0 fusion.287
  99.7 2.0 fusion.288
  101.9 34.5 %while.29 = (s32[]{:T(128)}, f32[6,32,2,128]{3,0,2,1:T(8,128)S(1)}, f32[128,128]{1,0:T(8,128)S(1)}, s32[]{:T(128)}, bf16[6,32,2,128]{3,1,2,0:T(8,128)(2,1)S(1)},...) while((s32[]{:T(128)}, f32[6,32,2,128]{3,0,2,1:T(8,128)S(1)}, ...), condition=%wide.region_5.6_spmd.clone, body=%wide.region_4.5_spmd.clone.sunk | while | flops 544574080 | bytes 70409384 | solution.py:153
  105.1 3.1 fusion.474
  109.2 5.0 subtract_multiply_fusion.4
  116.9 1.9 constant_dynamic-slice_fusion.6
  120.1 1.7 copy-done.1
  121.8 3.7 fusion.477
  126.2 5.2 fusion.478
  137.5 3.5 convolution_bitcast_fusion.2
  140.9 2.2 pad_maximum_fusion
  145.1 423.9 %all-reduce.10.cloned.1.call-done = f32[32,2,128,128]{3,2,0,1:T(8,128)} async-done(((f32[32,2,128,128]{3,2,0,1:T(8,128)}), f32[32,2,128,128]{3,2,0,1:T(8,128)}) %all-reduce.10.cloned.1.call-update) | async-done | bytes 4194320
  569.0 1.7 constant_dynamic-slice_fusion.2
  571.3 127.2 %all-reduce.6.cloned.1.call-done = f32[2,2,128,128]{3,2,0,1:T(8,128)} async-done(((f32[2,2,128,128]{3,2,0,1:T(8,128)}), f32[2,2,128,128]{3,2,0,1:T(8,128)}) %all-reduce.6.cloned.1.call-update) | async-done | bytes 262160 | tf_op jit(solution)/shard_map/psum | solution.py:157
  698.5 1.7 copy.102
  700.1 246.9 %all-reduce.8.cloned.1.call-done = f32[128,128]{1,0:T(8,128)} async-done(((f32[128,128]{1,0:T(8,128)}), f32[128,128]{1,0:T(8,128)}) %all-reduce.8.cloned.1.call-update) | async-done | bytes 65552 | tf_op jit(solution)/shard_map/psum | solution.py:158
  947.1 1.5 copy.274
  (85 shorter events, 16.9 us)
Async XLA Ops:
  7.2 90.6 %all-gather.2.cloned.1.call-start = ((), (), s32[]{:S(2)}) async-start(), calls=%async_computation | async-start | bytes 2228224 | tf_op jit(solution)/shard_map/all_gather | solution.py:123
  7.9 561.1 %all-reduce.10.cloned.1.call-start = ((), (), s32[]{:S(2)}) async-start(), calls=%async_computation.3 | async-start | bytes 8388608
  9.2 11.1 %copy-start.5 = (s32[16]{0:T(128)S(1)}, s32[16]{0:T(128)}, u32[]{:S(2)}) copy-start(s32[16]{0:T(128)} %param.15) | copy-start | bytes 196
  20.3 79.5 %copy-start.8 = (bf16[2]{0:T(256)(128)(2,1)S(1)}, bf16[2]{0:T(256)(128)(2,1)}, u32[]{:S(2)}) copy-start(bf16[2]{0:T(256)(128)(2,1)} %constant.200.clone) | copy-start | bytes 16
  91.5 10.5 %copy-start.3 = (bf16[128,128]{1,0:T(8,128)(2,1)S(1)}, bf16[128,128]{1,0:T(8,128)(2,1)}, u32[]{:S(2)}) copy-start(bf16[128,128]{1,0:T(8,128)(2,1)} %param.17) | copy-start | bytes 98308
  91.5 10.4 %copy-start.4 = (f32[128]{0:T(128)S(1)}, f32[128]{0:T(128)}, u32[]{:S(2)}) copy-start(f32[128]{0:T(128)} %param.18) | copy-start | bytes 1540
  91.5 10.4 %copy-start.6 = (s32[6]{0:T(128)S(1)}, s32[6]{0:T(128)}, u32[]{:S(2)}) copy-start(s32[6]{0:T(128)} %get-tuple-element.573) | copy-start | bytes 76
  116.9 2.5 copy-start
  120.0 1.7 copy-start.1
  136.4 6.8 copy-start.2
  143.2 0.7 copy-start.7
  143.2 555.3 %all-reduce.6.cloned.1.call-start = ((), (), s32[]{:S(2)}) async-start(), calls=%async_computation.1 | async-start | bytes 524288 | tf_op jit(solution)/shard_map/psum | solution.py:157
  570.7 376.4 %all-reduce.8.cloned.1.call-start = ((), (), s32[]{:S(2)}) async-start(), calls=%async_computation.2 | async-start | bytes 131072 | tf_op jit(solution)/shard_map/psum | solution.py:158
Sparse Core Ops, SparseCore 0:
  10.6 87.1 all-gather.1
  143.3 425.6 all-reduce.9
  572.2 126.2 all-reduce.5
  704.4 242.6 all-reduce.7
where the time goes:
time: 957 us; the launch traced here: 955 us
  waiting for transfers between devices  805 us (84%)
  blocking collectives  70.4 us (7%)
  matrix products  33.9 us (4%)
  between operations  15.3 us (2%)
  local copies, waits for them, and re-layouts  14 us (1%)
    unnamed x5, waiting for transfers between devices  425 us
    psum x1, waiting for transfers between devices, body(): grad_local = lax.psum(local_total, ('dp', 'fsdp'))  247 us
    psum x1, waiting for transfers between devices, body(): grad_spectral = lax.psum(grad_part, 'dp')  127 us
    psum x1, blocking collectives, body(): full_coeff = lax.psum(coeff_stack, 'fsdp')  70.4 us
  transfers between devices with their start and end apart: 4, of which 4 were waited for; matrix products, arithmetic and copies ran while one was open for 1% of the time, Pallas kernels for 0%

commit v1 on v0

--- a/solution.py
+++ b/solution.py
@@ -10,6 +10,12 @@
 highest = lax.Precision.HIGHEST
 root_half = 0.7071067811865476
 inv_root_two_pi = 0.3989422804014327
+
+
+def add_all(x, axis):
+    terms = lax.all_gather(x, axis, axis=0, tiled=False)
+    total = terms.sum(axis=0)
+    return total
 
 
 def phase_table(mode_ids, cell_ids, length, direction):
@@ -154,7 +160,7 @@
     grad_part = lax.psum_scatter(
         weight_grad(coeff_b, back_stack), "fsdp", scatter_dimension=0, tiled=True
     )
-    grad_spectral = lax.psum(grad_part, "dp")
+    grad_spectral = add_all(grad_part, "dp")
     grad_local = lax.psum(local_total, ("dp", "fsdp"))
     return (grad_spectral, grad_local)
 

time: 957 us -> 872 us (0.911)
  waiting for transfers between devices: 805 us -> 718 us
    psum x1 -> x0, waiting for transfers between devices: 127 us -> none  [body(): grad_spectral = lax.psum(grad_part, 'dp')]
    all_gather x0 -> x1, waiting for transfers between devices: none -> 43.5 us  [add_all(): terms = lax.all_gather(x, axis, axis=0, tiled=False)]
  transfers between devices with their start and end apart: 4 -> 4, of which waited for: 4 -> 4; matrix products, arithmetic and copies ran while one was open for 1% -> 2% of each run, Pallas kernels for 0% -> 0%
where the time goes in v1:
time: 872 us; the launch traced here: 870 us
  waiting for transfers between devices  718 us (82%)
  blocking collectives  70.4 us (8%)
  matrix products  33.9 us (4%)
  between operations  15.3 us (2%)
  local copies, waits for them, and re-layouts  13.1 us (2%)
  other arithmetic  11.4 us (1%)
    unnamed x5, waiting for transfers between devices  425 us
    psum x1, waiting for transfers between devices, body(): grad_local = lax.psum(local_total, ('dp', 'fsdp'))  244 us
    psum x1, blocking collectives, body(): full_coeff = lax.psum(coeff_stack, 'fsdp')  70.4 us
    all_gather x1, waiting for transfers between devices, add_all(): terms = lax.all_gather(x, axis, axis=0, tiled=False)  43.5 us
  transfers between devices with their start and end apart: 4, of which 4 were waited for; matrix products, arithmetic and copies ran while one was open for 2% of the time, Pallas kernels for 0%

profile of v1, /device:TPU:1, one launch (start us, length us, event | category | flops | bytes accessed | tf_op | source)
XLA Modules:
  0.0 870.2 jit_solution(8463158561614833300)
XLA Ops:
  7.9 1.2 dynamic_slice.42
  9.2 11.0 %while.28 = (s32[]{:T(128)}, f32[6,32,2,128]{3,0,2,1:T(8,128)S(1)}, s32[]{:T(128)}, s32[6]{0:T(128)}, bf16[6,3,48,48,128]{4,3,2,1,0:T(8,128)(2,1)}, /*index=5*/s32[]{:T(128)}, s32[]{:T(128)}, s32[]{:T(128)}, s32[]{:T(128)}) while((s32[]{:T(128)}, f32[6,32,2,128]{3,0,2,1:T(8,128)S(1)}, s32[]{:T(128)}, s32[6]{0:T(128)}, ...), condition=%wide.region_1.2_spmd.clone, body=%wide.region_0.0_spmd.clone.sunk | while | flops 14786103 | bytes 4907401 | solution.py:139
  9.9 1.3 dynamic_slice.73
  13.2 1.9 fusion.419
  15.4 1.9 fusion.421
  21.0 70.4 %all-reduce.8 = bf16[6,32,2,128]{3,0,2,1:T(8,128)(2,1)S(1)} all-reduce(f32[6,32,2,128]{3,0,2,1:T(8,128)S(1)} %get-tuple-element.239), channel_id=1, replica_groups=mesh['dp'=16,'fsdp'=16] {'fsdp'}, use_global_device_ids=true, to_apply=%region_2.3 | all-reduce | flops 49152 | bytes 294912 | tf_op jit(solution)/shard_map/psum | solution.py:140
  92.3 5.5 all-gather.4.cloned.1.call-done
  97.7 2.0 fusion.287
  99.7 2.0 fusion.288
  101.9 34.5 %while.29 = (s32[]{:T(128)}, f32[6,32,2,128]{3,0,2,1:T(8,128)S(1)}, f32[128,128]{1,0:T(8,128)S(1)}, s32[]{:T(128)}, bf16[6,32,2,128]{3,1,2,0:T(8,128)(2,1)S(1)},...) while((s32[]{:T(128)}, f32[6,32,2,128]{3,0,2,1:T(8,128)S(1)}, ...), condition=%wide.region_5.6_spmd.clone, body=%wide.region_4.5_spmd.clone.sunk | while | flops 544574080 | bytes 70409384 | solution.py:159
  105.1 3.1 fusion.474
  109.2 5.0 subtract_multiply_fusion.4
  116.9 1.9 constant_dynamic-slice_fusion.6
  120.1 1.7 copy-done.1
  121.8 3.7 fusion.477
  126.3 5.2 fusion.478
  137.5 3.5 convolution_bitcast_fusion.2
  140.9 2.2 pad_maximum_fusion
  145.1 423.9 %all-reduce.7.cloned.1.call-done = f32[32,2,128,128]{3,2,0,1:T(8,128)} async-done(((f32[32,2,128,128]{3,2,0,1:T(8,128)}), f32[32,2,128,128]{3,2,0,1:T(8,128)}) %all-reduce.7.cloned.1.call-update) | async-done | bytes 4194320
  569.0 1.7 constant_dynamic-slice_fusion.2
  571.3 43.5 %all-gather.6.cloned.1.call-done = f32[32,2,128,128]{3,2,0,1:T(8,128)} async-done(((f32[2,2,128,128]{3,2,0,1:T(8,128)}), f32[32,2,128,128]{3,2,0,1:T(8,128)}) %all-gather.6.cloned.1.call-update) | async-done | bytes 4194320 | tf_op jit(solution)/shard_map/all_gather | solution.py:16
  614.8 2.4 reduce_sum.19
  617.9 244.3 %all-reduce.5.cloned.1.call-done = f32[128,128]{1,0:T(8,128)} async-done(((f32[128,128]{1,0:T(8,128)}), f32[128,128]{1,0:T(8,128)}) %all-reduce.5.cloned.1.call-update) | async-done | bytes 65552 | tf_op jit(solution)/shard_map/psum | solution.py:164
  862.2 1.5 copy.273
  (86 shorter events, 17.6 us)
Async XLA Ops:
  7.2 90.6 %all-gather.4.cloned.1.call-start = ((), (), s32[]{:S(2)}) async-start(), calls=%async_computation | async-start | bytes 2228224 | tf_op jit(solution)/shard_map/all_gather | solution.py:129
  7.9 561.1 %all-reduce.7.cloned.1.call-start = ((), (), s32[]{:S(2)}) async-start(), calls=%async_computation.3 | async-start | bytes 8388608
  9.2 11.1 %copy-start.5 = (s32[16]{0:T(128)S(1)}, s32[16]{0:T(128)}, u32[]{:S(2)}) copy-start(s32[16]{0:T(128)} %param.15) | copy-start | bytes 196
  20.3 79.5 %copy-start.8 = (bf16[2]{0:T(256)(128)(2,1)S(1)}, bf16[2]{0:T(256)(128)(2,1)}, u32[]{:S(2)}) copy-start(bf16[2]{0:T(256)(128)(2,1)} %constant.201.clone) | copy-start | bytes 16
  91.5 10.5 %copy-start.3 = (bf16[128,128]{1,0:T(8,128)(2,1)S(1)}, bf16[128,128]{1,0:T(8,128)(2,1)}, u32[]{:S(2)}) copy-start(bf16[128,128]{1,0:T(8,128)(2,1)} %param.17) | copy-start | bytes 98308
  91.5 10.4 %copy-start.4 = (f32[128]{0:T(128)S(1)}, f32[128]{0:T(128)}, u32[]{:S(2)}) copy-start(f32[128]{0:T(128)} %param.18) | copy-start | bytes 1540
  91.5 10.4 %copy-start.6 = (s32[6]{0:T(128)S(1)}, s32[6]{0:T(128)}, u32[]{:S(2)}) copy-start(s32[6]{0:T(128)} %get-tuple-element.569) | copy-start | bytes 76
  116.9 2.5 copy-start
  120.1 1.7 copy-start.1
  136.4 6.8 copy-start.2
  143.2 0.7 copy-start.7
  143.2 471.6 %all-gather.6.cloned.1.call-start = ((), (), s32[]{:S(2)}) async-start(), calls=%async_computation.2 | async-start | bytes 4456448 | tf_op jit(solution)/shard_map/all_gather | solution.py:16
  570.7 291.5 %all-reduce.5.cloned.1.call-start = ((), (), s32[]{:S(2)}) async-start(), calls=%async_computation.1 | async-start | bytes 131072 | tf_op jit(solution)/shard_map/psum | solution.py:164
Sparse Core Ops, SparseCore 0:
  10.6 87.1 all-gather.3
  143.3 425.6 all-reduce.6
  571.4 43.3 all-gather.5
  620.7 241.4 all-reduce.4
